TPU v7x, 32 devices: a whole 2x2x4 slice. The times are simulated.
32 devices in a mesh: dp: 8 (over z, x), tensor: 4 (over y, core).
Axes of the slice: x: 2, y: 2, z: 4, core: 2. Of those that a mesh axis runs over, the one named last changes fastest.
Arguments:
- block_input: bfloat16 [8192, 1536], P(('dp', 'tensor')), may hold values from -6 to 6
- gain_attention: float32 [1536], replicated, may hold values from 0.1 to 1.9
- gain_feedforward: float32 [1536], replicated, may hold values from 0.1 to 1.9
- w_query: bfloat16 [1536, 1536], P(None, 'tensor'), as said below
- w_key: bfloat16 [1536, 768], P(None, 'tensor'), as said below
- w_value: bfloat16 [1536, 768], P(None, 'tensor'), may hold values from -0.15625 to 0.15625
- w_output: bfloat16 [1536, 1536], P('tensor'), may hold values from -1.25 to 1.25
- w_gate: bfloat16 [1536, 4096], P(None, 'tensor'), may hold values from -0.15625 to 0.15625
- w_up: bfloat16 [1536, 4096], P(None, 'tensor'), may hold values from -0.15625 to 0.15625
- w_down: bfloat16 [4096, 1536], P('tensor'), may hold values from -0.09375 to 0.09375
- cotangent: bfloat16 [8192, 1536], P(('dp', 'tensor')), may hold values from -12 to 12
Outputs:
- block_output: bfloat16 [8192, 1536], P(('dp', 'tensor'))
- input_grad: bfloat16 [8192, 1536], P(('dp', 'tensor'))
- grad_gain_attention: float32 [1536], replicated
- grad_gain_feedforward: float32 [1536], replicated
- grad_query: float32 [1536, 1536], P(None, 'tensor')
- grad_key: float32 [1536, 768], P(None, 'tensor')
- grad_value: float32 [1536, 768], P(None, 'tensor')
- grad_output: float32 [1536, 1536], P('tensor')
- grad_gate: float32 [1536, 4096], P(None, 'tensor')
- grad_up: float32 [1536, 4096], P(None, 'tensor')
- grad_down: float32 [4096, 1536], P('tensor')
Inputs may be any that keep to these rules, and one draw needn't show every extreme that they name: `w_query`: query projection. `w_key`: key projection with entries of order 1536^-0.5.
All inputs are finite; a program needn't handle non-finite values.
Results may differ from a plain program's by a relative error of at most 0.02.
Values may be sent and summed in bfloat16 or wider, within the bound.
No kernel may reach another device: no remote copies, remote signals or barrier semaphores. Data moves between devices by JAX's collectives and lax.ppermute only.
A program may use at most 192 MiB of HBM per device.

v0:
```python
import jax
import jax.numpy as jnp
from jax import lax
from jax.sharding import PartitionSpec as P

HD = 96
L = 1024
EPS = 1e-05
THETA = 100000.0


def rope_tables(length, width):
    position = jnp.arange(length, dtype=jnp.float32)[:, None]
    inverse = THETA ** (-jnp.arange(0, width, 2, dtype=jnp.float32) / width)
    angles = position * inverse[None, :]
    angles = jnp.concatenate([angles, angles], axis=-1)
    return (jnp.cos(angles), jnp.sin(angles))


def rotate(values_in, cosine, sine):
    half_width = values_in.shape[-1] // 2
    turned = jnp.concatenate([-values_in[..., half_width:], values_in[..., :half_width]], axis=-1)
    return values_in * cosine[:, None, :] + turned * sine[:, None, :]


def unrotate(grad_in, cosine, sine):
    half_width = grad_in.shape[-1] // 2
    scaled = grad_in * sine[:, None, :]
    turned = jnp.concatenate([scaled[..., half_width:], -scaled[..., :half_width]], axis=-1)
    return grad_in * cosine[:, None, :] + turned


def norm_forward(inputs, gain):
    recip = lax.rsqrt(jnp.mean(inputs * inputs, axis=-1, keepdims=True) + EPS)
    return ((inputs * recip * gain).astype(jnp.bfloat16), recip)


def norm_backward(inputs, recip, gain, dnormed):
    scaled = gain * dnormed
    gain_part = jnp.sum(dnormed * inputs * recip, axis=0)
    inner = jnp.mean(scaled * inputs, axis=-1, keepdims=True)
    return (gain_part, recip * scaled - inputs * recip * recip * recip * inner)


def outer_sum(left, right):
    return lax.dot_general(
        left, right, (((0,), (0,)), ((), ())), preferred_element_type=jnp.float32
    )


def times_transpose(left, weight):
    return lax.dot_general(
        left, weight, (((1,), (1,)), ((), ())), preferred_element_type=jnp.float32
    )


def masked_scores(query, keys):
    length = query.shape[0]
    scores = jnp.einsum("lkgd,mkd->kglm", query, keys, preferred_element_type=jnp.float32) * HD ** (
        -0.5
    )
    causal = lax.broadcasted_iota(jnp.int32, (length, length), 0) >= lax.broadcasted_iota(
        jnp.int32, (length, length), 1
    )
    return jnp.where(causal, scores, -jnp.inf)


def attend(query, keys, values):
    scores = masked_scores(query, keys)
    row_max = jnp.max(scores, axis=-1, keepdims=True)
    exponent = jnp.exp(scores - row_max)
    row_total = jnp.sum(exponent, axis=-1, keepdims=True)
    probability = (exponent / row_total).astype(jnp.bfloat16)
    log_total = row_max + jnp.log(row_total)
    attended = jnp.einsum("kglm,mkd->lkgd", probability, values, preferred_element_type=jnp.float32)
    return (attended.astype(jnp.bfloat16), log_total)


def attend_back(query, keys, values, attended, log_total, dattended):
    scores = masked_scores(query, keys)
    probability = jnp.exp(scores - log_total)
    prob_rounded = probability.astype(jnp.bfloat16)
    value_grad = jnp.einsum(
        "kglm,lkgd->mkd", prob_rounded, dattended, preferred_element_type=jnp.float32
    )
    dprob = jnp.einsum("lkgd,mkd->kglm", dattended, values, preferred_element_type=jnp.float32)
    delta = jnp.sum(dattended.astype(jnp.float32) * attended.astype(jnp.float32), axis=-1)
    delta = jnp.transpose(delta, (1, 2, 0))[..., None]
    dscore = (probability * (dprob - delta)).astype(jnp.bfloat16)
    query_grad = jnp.einsum(
        "kglm,mkd->lkgd", dscore, keys, preferred_element_type=jnp.float32
    ) * HD ** (-0.5)
    key_grad = jnp.einsum(
        "kglm,lkgd->mkd", dscore, query, preferred_element_type=jnp.float32
    ) * HD ** (-0.5)
    return (query_grad, key_grad, value_grad)


def body(
    block_input,
    gain_attention,
    gain_feedforward,
    w_query,
    w_key,
    w_value,
    w_output,
    w_gate,
    w_up,
    w_down,
    cotangent,
):
    query_cols = w_query.shape[1]
    pair_cols = w_key.shape[1]
    query_heads = query_cols // HD
    pair_heads = pair_cols // HD
    inputs = block_input.astype(jnp.float32)
    normed_one, recip_one = norm_forward(inputs, gain_attention)
    full_one = lax.all_gather(normed_one, "tensor", axis=0, tiled=True)
    rows_all = full_one.shape[0]
    sequences = rows_all // L
    cosine, sine = rope_tables(L, HD)
    query = jnp.dot(full_one, w_query, preferred_element_type=jnp.float32).reshape(
        sequences, L, query_heads, HD
    )
    query = (
        rotate(query, cosine, sine).astype(jnp.bfloat16).reshape(sequences, L, pair_heads, 2, HD)
    )
    keys = jnp.dot(full_one, w_key, preferred_element_type=jnp.float32).reshape(
        sequences, L, pair_heads, HD
    )
    keys = rotate(keys, cosine, sine).astype(jnp.bfloat16)
    values = (
        jnp.dot(full_one, w_value, preferred_element_type=jnp.float32)
        .astype(jnp.bfloat16)
        .reshape(sequences, L, pair_heads, HD)
    )
    attended, log_total = lax.map(
        lambda members: attend(members[0], members[1], members[2]), (query, keys, values)
    )
    flat_attended = attended.reshape(rows_all, query_cols)
    resid = inputs + lax.psum_scatter(
        jnp.dot(flat_attended, w_output, preferred_element_type=jnp.float32).astype(jnp.bfloat16),
        "tensor",
        scatter_dimension=0,
        tiled=True,
    ).astype(jnp.float32)
    normed_two, recip_two = norm_forward(resid, gain_feedforward)
    full_two = lax.all_gather(normed_two, "tensor", axis=0, tiled=True)
    gate = jnp.dot(full_two, w_gate, preferred_element_type=jnp.float32)
    up_proj = jnp.dot(full_two, w_up, preferred_element_type=jnp.float32)
    sigmoid_gate = jax.nn.sigmoid(gate)
    activated = gate * sigmoid_gate
    hidden = (activated * up_proj).astype(jnp.bfloat16)
    block_output = (
        resid
        + lax.psum_scatter(
            jnp.dot(hidden, w_down, preferred_element_type=jnp.float32).astype(jnp.bfloat16),
            "tensor",
            scatter_dimension=0,
            tiled=True,
        ).astype(jnp.float32)
    ).astype(jnp.bfloat16)
    full_grad = lax.all_gather(cotangent, "tensor", axis=0, tiled=True)
    grad_down = outer_sum(hidden, full_grad)
    dhidden = times_transpose(full_grad, w_down)
    dgate = (dhidden * up_proj * sigmoid_gate * (1.0 + gate * (1.0 - sigmoid_gate))).astype(
        jnp.bfloat16
    )
    dup_proj = (dhidden * activated).astype(jnp.bfloat16)
    grad_gate = outer_sum(full_two, dgate)
    grad_up = outer_sum(full_two, dup_proj)
    dnormed_two = lax.psum_scatter(
        (times_transpose(dgate, w_gate) + times_transpose(dup_proj, w_up)).astype(jnp.bfloat16),
        "tensor",
        scatter_dimension=0,
        tiled=True,
    ).astype(jnp.float32)
    gain_two_part, dresid_norm = norm_backward(resid, recip_two, gain_feedforward, dnormed_two)
    dresid = cotangent.astype(jnp.float32) + dresid_norm
    full_dresid = lax.all_gather(dresid.astype(jnp.bfloat16), "tensor", axis=0, tiled=True)
    grad_output = outer_sum(flat_attended, full_dresid)
    dattended = (
        times_transpose(full_dresid, w_output)
        .astype(jnp.bfloat16)
        .reshape(sequences, L, pair_heads, 2, HD)
    )
    query_grad, key_grad, value_grad = lax.map(
        lambda members: attend_back(
            members[0], members[1], members[2], members[3], members[4], members[5]
        ),
        (query, keys, values, attended, log_total, dattended),
    )
    query_grad = (
        unrotate(query_grad.reshape(sequences, L, query_heads, HD), cosine, sine)
        .astype(jnp.bfloat16)
        .reshape(rows_all, query_cols)
    )
    key_grad = unrotate(key_grad, cosine, sine).astype(jnp.bfloat16).reshape(rows_all, pair_cols)
    value_grad = value_grad.astype(jnp.bfloat16).reshape(rows_all, pair_cols)
    grad_query = outer_sum(full_one, query_grad)
    grad_key = outer_sum(full_one, key_grad)
    grad_value = outer_sum(full_one, value_grad)
    term = times_transpose(query_grad, w_query)
    term = term + times_transpose(key_grad, w_key)
    dnormed_one = lax.psum_scatter(
        (term + times_transpose(value_grad, w_value)).astype(jnp.bfloat16),
        "tensor",
        scatter_dimension=0,
        tiled=True,
    ).astype(jnp.float32)
    gain_one_part, dinput_norm = norm_backward(inputs, recip_one, gain_attention, dnormed_one)
    input_grad = (dresid + dinput_norm).astype(jnp.bfloat16)
    grad_gain_one, grad_gain_two = lax.psum((gain_one_part, gain_two_part), ("dp", "tensor"))
    grad_output, grad_query, grad_key, grad_value, grad_gate, grad_up, grad_down = (
        lax.psum(grad_output.astype(jnp.bfloat16), "dp").astype(jnp.float32),
        lax.psum(grad_query.astype(jnp.bfloat16), "dp").astype(jnp.float32),
        lax.psum(grad_key.astype(jnp.bfloat16), "dp").astype(jnp.float32),
        lax.psum(grad_value.astype(jnp.bfloat16), "dp").astype(jnp.float32),
        lax.psum(grad_gate.astype(jnp.bfloat16), "dp").astype(jnp.float32),
        lax.psum(grad_up.astype(jnp.bfloat16), "dp").astype(jnp.float32),
        lax.psum(grad_down.astype(jnp.bfloat16), "dp").astype(jnp.float32),
    )
    return (
        block_output,
        input_grad,
        grad_gain_one,
        grad_gain_two,
        grad_query,
        grad_key,
        grad_value,
        grad_output,
        grad_gate,
        grad_up,
        grad_down,
    )


def solution(mesh):
    placed = (
        P(("dp", "tensor"), None),
        P(),
        P(),
        P(None, "tensor"),
        P(None, "tensor"),
        P(None, "tensor"),
        P("tensor", None),
        P(None, "tensor"),
        P(None, "tensor"),
        P("tensor", None),
        P(("dp", "tensor"), None),
    )
    return jax.shard_map(
        body,
        mesh=mesh,
        in_specs=placed,
        out_specs=(
            P(("dp", "tensor"), None),
            P(("dp", "tensor"), None),
            P(),
            P(),
            P(None, "tensor"),
            P(None, "tensor"),
            P(None, "tensor"),
            P("tensor", None),
            P(None, "tensor"),
            P(None, "tensor"),
            P("tensor", None),
        ),
        check_vma=False,
    )
```

profile of v0, /device:TPU:0, one launch (start us, length us, event | category | flops | bytes accessed | tf_op | source)
XLA Modules:
  0.0 811.2 jit_solution(7775134368866438504)
XLA Ops:
  7.2 1.5 fusion.26
  8.8 0.6 copy-done.39
  9.3 2.3 fusion.15
  11.8 2.3 broadcast_multiply_fusion.1
  14.0 1.3 iota_compare_fusion
  15.3 27.7 %all-gather.5.cloned.1.call-done = bf16[1024,1536]{1,0:T(8,128)(2,1)} async-done(((bf16[256,1536]{1,0:T(8,128)(2,1)}), bf16[1024,1536]{1,0:T(8,128)(2,1)}) %all-gather.5.cloned.1.call-update) | async-done | bytes 3145744 | tf_op jit(solution)/shard_map/all_gather | solution.py:118
  43.0 3.3 fusion.55
  46.4 1.4 fusion.56
  48.1 0.8 copy-done.4
  49.6 0.7 copy-done.6
  50.3 3.1 fusion.4
  53.4 3.7 fusion.2
  57.1 1.2 convolution_convert_fusion.10
  58.3 0.9 copy-done.1
  59.2 5.1 fusion.34
  64.3 0.9 copy-done.24
  65.2 3.5 convolution_convert_fusion
  68.9 37.8 %reduce-scatter.5.cloned.1.call-done = bf16[256,1536]{1,0:T(8,128)(2,1)} async-done(((bf16[1024,1536]{1,0:T(8,128)(2,1)}), bf16[256,1536]{1,0:T(8,128)(2,1)}) %reduce-scatter.5.cloned.1.call-update) | async-done | bytes 786448 | tf_op jit(solution)/shard_map/reduce_scatter | solution.py:141
  106.7 1.7 multiply_reduce_fusion.1
  108.5 0.6 copy-done.36
  109.0 2.5 multiply_convert_fusion.3
  112.2 28.0 %all-gather.7.cloned.1.call-done = bf16[1024,1536]{1,0:T(8,128)(2,1)} async-done(((bf16[256,1536]{1,0:T(8,128)(2,1)}), bf16[1024,1536]{1,0:T(8,128)(2,1)}) %all-gather.7.cloned.1.call-update) | async-done | bytes 3145744 | tf_op jit(solution)/shard_map/all_gather | solution.py:148
  140.3 8.4 %fusion.58 = f32[1024,1024]{1,0:T(8,128)} fusion(bf16[1024,1536]{1,0:T(8,128)(2,1)} %all-gather.7.cloned.1.call-done, bf16[1536,1024]{1,0:T(8,128)(2,1)} %param.19), kind=kOutput, calls=%fused_computation.113 | convolution fusion | flops 3221225472 | bytes 10485760 | tf_op jit(solution)/shard_map/dot_general | solution.py:150
  148.7 4.9 fusion.57
  153.6 16.6 %all-gather.9.cloned.1.call-done = bf16[1024,1536]{1,0:T(8,128)(2,1)} async-done(((bf16[256,1536]{1,0:T(8,128)(2,1)}), bf16[1024,1536]{1,0:T(8,128)(2,1)}) %all-gather.9.cloned.1.call-update) | async-done | bytes 3145744 | tf_op jit(solution)/shard_map/all_gather | solution.py:163
  170.2 9.5 %multiply_convert_fusion = (bf16[1024,1024]{1,0:T(8,128)(2,1)S(1)}, bf16[1024,1024]{1,0:T(8,128)(2,1)S(1)}, bf16[1024,1024]{1,0:T(8,128)(2,1)}) fusion(f32[1024,1024]{1,0:T(8,128)} %fusion.57, f32[1024,1024]{1,0:T(8,128)} %fusion.58, bf16[1024,1536]{1,0:T(8,128)(2,1)} %all-gather.9.cloned.1.call-done, bf16[1024,1536]{1,0:T(8,128)(2,1)S(1)} %copy-done), kind=kOutput, calls=%fused_computation.15 | convolution fusion | flops 3236954112 | bytes 20971520 | tf_op jit(solution)/shard_map/dot_general | solution.py:52
  179.8 3.5 fusion.59
  183.3 4.9 add_convert_fusion.1
  188.2 38.0 %reduce-scatter.9.cloned.1.call-done = bf16[256,1536]{1,0:T(8,128)(2,1)} async-done(((bf16[1024,1536]{1,0:T(8,128)(2,1)}), bf16[256,1536]{1,0:T(8,128)(2,1)}) %reduce-scatter.9.cloned.1.call-update) | async-done | bytes 786448 | tf_op jit(solution)/shard_map/reduce_scatter | solution.py:172
  226.2 2.2 fusion.25
  228.4 0.5 copy-done.41
  228.9 3.4 fusion.53
  232.8 1.4 log_add_fusion
  234.2 26.9 %all-gather.11.cloned.1.call-done = bf16[1024,1536]{1,0:T(8,128)(2,1)} async-done(((bf16[256,1536]{1,0:T(8,128)(2,1)}), bf16[1024,1536]{1,0:T(8,128)(2,1)}) %all-gather.11.cloned.1.call-update) | async-done | bytes 3145744 | tf_op jit(solution)/shard_map/all_gather | solution.py:180
  261.1 3.8 convolution_convert_fusion.9
  265.2 8.2 %fusion.38 = bf16[2,96,1024]{2,1,0:T(8,128)(2,1)S(1)} fusion(bf16[1024,2,2,96]{0,3,2,1:T(8,128)(2,1)S(1)} %bitcast.151, f32[2,1024,1024,2]{2,1,3,0:T(8,128)} %copy-done.1, f32[2,2,1024]{2,1,0:T(2,128)S(1)} %copy-done.38, pred[1024,1024]{0,1:T(8,128)(4,1)S(1)} %copy-done.7), kind=kOutput, calls=%fused_computation.76 | convolution fusion | flops 822280192 | bytes 19021824 | tf_op jit(solution)/shard_map/while/body/eval_jaxpr/kglm,lkgd->mkd/dot_general | solution.py:83
  273.4 9.5 %fusion.1 = bf16[2,2,1024,1024]{2,3,1,0:T(8,128)(2,1)S(1)} fusion(f32[2,1024,1024,2]{2,1,3,0:T(8,128)} %copy-done.1, f32[2,2,1024]{2,1,0:T(2,128)S(1)} %bitcast.153, f32[2,2,1024]{2,1,0:T(2,128)S(1)} %copy-done.38, pred[1024,1024]{0,1:T(8,128)(4,1)S(1)} %copy-done.7, bf16[1024,2,96,1]{0,2,3,1:T(8,128)(2,1)S(1)} %bitcast.155, ...), kind=kOutput, calls=%fused_computation.2 | convolution fusion | flops 830472192 | bytes 27426816 | tf_op jit(solution)/shard_map/while/body/eval_jaxpr/lkgd,mkd->kglm/dot_general | solution.py:86
  282.9 2.7 convolution_bitcast_fusion
  285.7 1.5 convolution_multiply_fusion
  287.3 0.8 copy-done.5
  289.1 0.7 copy-done.22
  289.8 1.9 fusion.60
  291.9 1.0 fusion.61
  292.9 2.7 add_convert_fusion
  295.8 6.4 convolution_convert_fusion.4
  302.4 8.6 %convolution_convert_fusion.1 = bf16[1024,1536]{1,0:T(8,128)(2,1)} fusion(bf16[1024,1024]{1,0:T(8,128)(2,1)} %get-tuple-element.74, bf16[1024,1536]{1,0:T(8,128)(2,1)} %all-gather.9.cloned.1.call-done), kind=kOutput, calls=%fused_computation.22 | convolution fusion | flops 3222798336 | bytes 8388608 | tf_op jit(solution)/shard_map/dot_general | solution.py:46
  311.0 4.9 convolution_convert_fusion.2
  315.9 4.8 convolution_convert_fusion.3
  320.8 1.6 convolution_convert_fusion.8
  322.4 1.6 convolution_convert_fusion.7
  324.0 2.4 convolution_convert_fusion.5
  326.4 2.9 convolution_convert_fusion.6
  329.3 4.5 reduce-scatter.11.cloned.1.call-done
  333.8 1.8 fusion.29
  335.6 40.0 %all-reduce = (f32[1536]{0:T(1024)}, f32[1536]{0:T(1024)}) all-reduce(f32[1536]{0:T(1024)S(1)} %get-tuple-element.51, f32[1536]{0:T(1024)S(1)} %get-tuple-element.49), channel_id=1, replica_groups=mesh['dp'=8,'tensor'=4] {'dp','tensor'}, use_global_device_ids=true, to_apply=%region_12.13 | all-reduce | flops 3072 | bytes 24576 | tf_op jit(solution)/shard_map/psum | solution.py:213
  375.6 4.9 fusion.20
  380.5 406.2 %all-reduce.4.cloned.1.call-done = (bf16[1536,384]{1,0:T(8,128)(2,1)}, bf16[1536,192]{0,1:T(8,128)(2,1)}, bf16[1536,192]{0,1:T(8,128)(2,1)}, bf16[384,1536]{1,0:...) async-done(((bf16[1536,384]{1,0:T(8,128)(2,1)}, bf16[1536,192]{0,1:T(8,128)(2,1)}, bf16[1536,192]{0,1:T(8,128)(2,1)}, ...) | async-done | bytes 12976144 | tf_op jit(solution)/shard_map/psum | solution.py:216
  786.7 3.0 convert_element_type.192
  789.7 1.1 convert_element_type.194
  790.9 1.1 convert_element_type.196
  792.0 1.7 convert_element_type.198
  793.7 3.5 convert_element_type.200
  797.2 3.5 convert_element_type.202
  800.6 3.6 convert_element_type.204
  (140 shorter events, 4.7 us)
Async XLA Ops:
  7.2 163.0 %copy-start = (bf16[1024,1536]{1,0:T(8,128)(2,1)S(1)}, bf16[1024,1536]{1,0:T(8,128)(2,1)}, u32[]{:S(2)}) copy-start(bf16[1024,1536]{1,0:T(8,128)(2,1)} %param.20) | copy-start | bytes 9437188
  7.2 35.8 %all-gather.5.cloned.1.call-start = ((), (), s32[]{:S(2)}) async-start(), calls=%async_computation.4 | async-start | bytes 3932160 | tf_op jit(solution)/shard_map/all_gather | solution.py:118
  8.8 0.6 copy-start.39
  11.6 95.1 %reduce-scatter.5.cloned.1.call-start = ((), (), s32[]{:S(2)}) async-start(), calls=%async_computation.5 | async-start | bytes 3932160 | tf_op jit(solution)/shard_map/reduce_scatter | solution.py:141
  43.0 3.4 copy-start.2
  43.0 3.4 copy-start.21
  47.9 1.0 copy-start.4
  48.9 1.4 copy-start.6
  49.1 4.2 copy-start.15
  50.3 3.1 copy-start.10
  53.4 5.8 copy-start.1
  53.4 5.8 copy-start.34
  53.4 3.7 copy-start.27
  57.1 7.1 copy-start.35
  58.3 6.0 copy-start.50
  59.2 6.0 copy-start.49
  64.3 0.9 copy-start.24
  68.7 40.4 %copy-start.32 = (f32[1536]{0:T(1024)S(1)}, f32[1536]{0:T(1024)}, u32[]{:S(2)}) copy-start(f32[1536]{0:T(1024)} %param.13) | copy-start | bytes 18436
  68.7 71.6 %all-gather.7.cloned.1.call-start = ((), (), s32[]{:S(2)}) async-start(), calls=%async_computation.6 | async-start | bytes 3932160 | tf_op jit(solution)/shard_map/all_gather | solution.py:148
  108.4 0.6 copy-start.36
  111.6 58.6 %all-gather.9.cloned.1.call-start = ((), (), s32[]{:S(2)}) async-start(), calls=%async_computation.8 | async-start | bytes 3932160 | tf_op jit(solution)/shard_map/all_gather | solution.py:163
  112.2 114.0 %reduce-scatter.9.cloned.1.call-start = ((), (), s32[]{:S(2)}) async-start(), calls=%async_computation.9 | async-start | bytes 3932160 | tf_op jit(solution)/shard_map/reduce_scatter | solution.py:172
  140.3 8.4 %copy-start.43 = (bf16[1536,1024]{1,0:T(8,128)(2,1)S(1)}, bf16[1536,1024]{1,0:T(8,128)(2,1)}, u32[]{:S(2)}) copy-start(bf16[1536,1024]{1,0:T(8,128)(2,1)} %param.18) | copy-start | bytes 9437188
  140.3 8.4 %copy-start.46 = (bf16[1024,1536]{1,0:T(8,128)(2,1)S(1)}, bf16[1024,1536]{1,0:T(8,128)(2,1)}, u32[]{:S(2)}) copy-start(bf16[1024,1536]{1,0:T(8,128)(2,1)} %all-gather.7.cloned.1.call-done) | copy-start | bytes 9437188
  170.2 9.5 %copy-start.44 = (bf16[1536,1024]{1,0:T(8,128)(2,1)S(1)}, bf16[1536,1024]{1,0:T(8,128)(2,1)}, u32[]{:S(2)}) copy-start(bf16[1536,1024]{1,0:T(8,128)(2,1)} %param.18) | copy-start | bytes 9437188
  179.7 3.5 copy-start.52
  179.7 3.5 copy-start.54
  179.7 3.5 copy-start.45
  188.2 72.9 %all-gather.11.cloned.1.call-start = ((), (), s32[]{:S(2)}) async-start(), calls=%async_computation.10 | async-start | bytes 3932160 | tf_op jit(solution)/shard_map/all_gather | solution.py:180
  232.4 101.4 %reduce-scatter.11.cloned.1.call-start = ((), (), s32[]{:S(2)}) async-start(), calls=%async_computation.11 | async-start | bytes 3932160 | tf_op jit(solution)/shard_map/reduce_scatter | solution.py:205
  261.1 3.8 copy-start.25
  261.1 4.1 copy-start.7
  261.1 4.1 copy-start.38
  265.2 8.3 %copy-start.51 = (bf16[1024,192]{0,1:T(8,128)(2,1)S(1)}, bf16[1024,192]{0,1:T(8,128)(2,1)}, u32[]{:S(2)}) copy-start(bf16[1024,192]{0,1:T(8,128)(2,1)} %copy-done.50) | copy-start | bytes 1179652
  273.4 19.5 %copy-start.19 = (bf16[2,96,1024]{2,1,0:T(8,128)(2,1)}, bf16[2,96,1024]{2,1,0:T(8,128)(2,1)S(1)}, u32[]{:S(2)}) copy-start(bf16[2,96,1024]{2,1,0:T(8,128)(2,1)S(1)} %fusion.38) | copy-start | bytes 1179652
  273.4 9.5 %copy-start.11 = (bf16[1024,2,2,96]{0,3,2,1:T(8,128)(2,1)S(1)}, bf16[1024,2,2,96]{0,3,2,1:T(8,128)(2,1)}, u32[]{:S(2)}) copy-start(bf16[1024,2,2,96]{0,3,2,1:T(8,128)(2,1)} %copy-done.10) | copy-start | bytes 2359300
  282.9 2.7 copy-start.16
  285.7 1.5 copy-start.18
  287.2 1.0 copy-start.5
  288.5 1.3 copy-start.22
  289.8 1.9 copy-start.8
  289.8 1.9 copy-start.17
  289.8 2.1 copy-start.31
  291.9 1.1 copy-start.28
  295.7 79.9 %reduce-scatter.7.cloned.1.call-start = ((), (), s32[]{:S(2)}) async-start(), calls=%async_computation.7 | async-start | bytes 3932160 | tf_op jit(solution)/shard_map/reduce_scatter | solution.py:156
  302.2 484.6 %all-reduce.4.cloned.1.call-start = ((), (), s32[]{:S(2)}) async-start(), calls=%async_computation.12 | async-start | bytes 25952256 | tf_op jit(solution)/shard_map/psum | solution.py:216
  302.4 8.6 %copy-start.47 = (bf16[1024,1536]{1,0:T(8,128)(2,1)S(1)}, bf16[1024,1536]{1,0:T(8,128)(2,1)}, u32[]{:S(2)}) copy-start(bf16[1024,1536]{1,0:T(8,128)(2,1)} %all-gather.7.cloned.1.call-done) | copy-start | bytes 9437188
  302.4 8.6 %copy-start.55 = (bf16[1024,1024]{1,0:T(8,128)(2,1)S(1)}, bf16[1024,1024]{1,0:T(8,128)(2,1)}, u32[]{:S(2)}) copy-start(bf16[1024,1024]{1,0:T(8,128)(2,1)} %copy-done.54) | copy-start | bytes 6291460
  311.0 4.9 copy-start.53
  315.9 4.9 copy-start.3
  320.8 1.6 copy-start.20
  320.8 3.2 copy-start.26
  320.8 3.2 copy-start.48
  324.0 2.4 copy-start.9
  329.3 4.5 copy-start.33
  329.3 4.5 copy-start.40
  329.3 46.3 %copy-start.37 = (f32[256]{0:T(256)S(1)}, f32[256]{0:T(256)}, u32[]{:S(2)}) copy-start(f32[256]{0:T(256)} %copy-done.36) | copy-start | bytes 3076
  329.3 46.3 %copy-start.42 = (f32[256]{0:T(256)S(1)}, f32[256]{0:T(256)}, u32[]{:S(2)}) copy-start(f32[256]{0:T(256)} %copy-done.41) | copy-start | bytes 3076
  786.7 3.0 copy-start.30
  786.7 4.1 copy-start.29
  786.7 5.3 copy-start.23
  789.7 4.0 copy-start.14
  793.7 3.5 copy-start.13
  797.2 3.5 copy-start.12
  (1 other events, 0.5 us)
Sparse Core Ops, SparseCore 0:
  11.7 31.2 all-gather.4
  68.8 37.8 reduce-scatter.4
  111.7 28.4 all-gather.6
  141.7 28.4 all-gather.8
  188.3 37.8 reduce-scatter.8
  232.5 28.4 all-gather.10
  295.8 37.8 reduce-scatter.10
  336.9 38.2 reduce-scatter.6
  382.0 404.7 all-reduce.3
where the time goes:
time: 820 us; the launch traced here: 811 us
  waiting for transfers between devices  586 us (71%)
  matrix products  113 us (14%)
  other arithmetic  49 us (6%)
  blocking collectives  40 us (5%)
  between operations  14.9 us (2%)
    psum x1, waiting for transfers between devices, body(): lax.psum(grad_query.astype(jnp.bfloat16), 'dp').astype(jnp.float32)  406 us
    psum x1, blocking collectives, body(): lax.psum((gain_one_part, gain_two_part), ('dp', 'tensor'))  40 us
    reduce_scatter x1, waiting for transfers between devices, body(): lax.psum_scatter((times_transpose(dgate, w_gate) + times_transpose(dup_pr...  38 us
    reduce_scatter x1, waiting for transfers between devices, body(): lax.psum_scatter(jnp.dot(flat_attended, w_output, preferred_element_type=...  37.8 us
    all_gather x1, waiting for transfers between devices, body(): full_two = lax.all_gather(normed_two, 'tensor', axis=0, tiled=True)  28 us
    all_gather x1, waiting for transfers between devices, body(): full_one = lax.all_gather(normed_one, 'tensor', axis=0, tiled=True)  27.7 us
    dot_general x7, matrix products, times_transpose(): lax.dot_general(left, weight, (((1,), (1,)), ((), ())), preferred_element...  27.2 us
    all_gather x1, waiting for transfers between devices, body(): lax.all_gather(dresid.astype(jnp.bfloat16), 'tensor', axis=0, tiled=True)  26.9 us
  transfers between devices with their start and end apart: 9, of which 8 were waited for; matrix products, arithmetic and copies ran while one was open for 7% of the time, Pallas kernels for 0%

commit v1 on v0

--- a/solution.py
+++ b/solution.py
@@ -213,7 +213,7 @@
     grad_gain_one, grad_gain_two = lax.psum((gain_one_part, gain_two_part), ("dp", "tensor"))
     grad_output, grad_query, grad_key, grad_value, grad_gate, grad_up, grad_down = (
         lax.psum(grad_output.astype(jnp.bfloat16), "dp").astype(jnp.float32),
-        lax.psum(grad_query.astype(jnp.bfloat16), "dp").astype(jnp.float32),
+        jnp.sum(lax.all_gather(grad_query.astype(jnp.bfloat16), "dp"), axis=0).astype(jnp.float32),
         lax.psum(grad_key.astype(jnp.bfloat16), "dp").astype(jnp.float32),
         lax.psum(grad_value.astype(jnp.bfloat16), "dp").astype(jnp.float32),
         lax.psum(grad_gate.astype(jnp.bfloat16), "dp").astype(jnp.float32),

time: 820 us -> 908 us (1.11)
  waiting for transfers between devices: 586 us -> 663 us
    all_gather x0 -> x1, waiting for transfers between devices: none -> 122 us  [body(): lax.all_gather(grad_query.astype(jnp.bfloat16), 'dp')]
    psum x1, waiting for transfers between devices: 406 us -> 364 us  [body(): lax.psum(grad_key.astype(jnp.bfloat16), 'dp').astype(jnp.float32)]
  transfers between devices with their start and end apart: 9 -> 10, of which waited for: 8 -> 9; matrix products, arithmetic and copies ran while one was open for 7% -> 9% of each run, Pallas kernels for 0% -> 0%
where the time goes in v1:
time: 908 us; the launch traced here: 899 us
  waiting for transfers between devices  663 us (73%)
  matrix products  115 us (13%)
  other arithmetic  57.8 us (6%)
  blocking collectives  40 us (4%)
  between operations  15.2 us (2%)
    psum x1, waiting for transfers between devices, body(): lax.psum(grad_key.astype(jnp.bfloat16), 'dp').astype(jnp.float32)  364 us
    all_gather x1, waiting for transfers between devices, body(): lax.all_gather(grad_query.astype(jnp.bfloat16), 'dp')  122 us
    psum x1, blocking collectives, body(): lax.psum((gain_one_part, gain_two_part), ('dp', 'tensor'))  40 us
    reduce_scatter x1, waiting for transfers between devices, body(): lax.psum_scatter((times_transpose(dgate, w_gate) + times_transpose(dup_pr...  38 us
    reduce_scatter x1, waiting for transfers between devices, body(): lax.psum_scatter(jnp.dot(flat_attended, w_output, preferred_element_type=...  37.8 us
    dot_general x7, matrix products, outer_sum(): lax.dot_general(left, right, (((0,), (0,)), ((), ())), preferred_element_...  29 us
    all_gather x1, waiting for transfers between devices, body(): full_two = lax.all_gather(normed_two, 'tensor', axis=0, tiled=True)  28 us
    all_gather x1, waiting for transfers between devices, body(): full_one = lax.all_gather(normed_one, 'tensor', axis=0, tiled=True)  27.7 us
  transfers between devices with their start and end apart: 10, of which 9 were waited for; matrix products, arithmetic and copies ran while one was open for 9% of the time, Pallas kernels for 0%

profile of v1, /device:TPU:0, one launch (start us, length us, event | category | flops | bytes accessed | tf_op | source)
XLA Modules:
  0.0 899.3 jit_solution(4656881589462226952)
XLA Ops:
  7.2 1.5 fusion.26
  9.3 2.3 fusion.15
  11.8 2.3 broadcast_multiply_fusion.1
  14.1 1.3 iota_compare_fusion
  15.3 27.7 %all-gather.7.cloned.1.call-done = bf16[1024,1536]{1,0:T(8,128)(2,1)} async-done(((bf16[256,1536]{1,0:T(8,128)(2,1)}), bf16[1024,1536]{1,0:T(8,128)(2,1)}) %all-gather.7.cloned.1.call-update) | async-done | bytes 3145744 | tf_op jit(solution)/shard_map/all_gather | solution.py:118
  43.0 3.3 fusion.55
  46.4 1.4 fusion.56
  48.1 0.8 copy-done.4
  49.6 0.7 copy-done.6
  50.3 3.1 fusion.4
  53.4 3.7 fusion.2
  57.1 1.2 convolution_convert_fusion.10
  58.3 0.9 copy-done.1
  59.2 5.1 fusion.34
  64.3 0.9 copy-done.23
  65.2 3.5 convolution_convert_fusion
  69.0 37.8 %reduce-scatter.5.cloned.1.call-done = bf16[256,1536]{1,0:T(8,128)(2,1)} async-done(((bf16[1024,1536]{1,0:T(8,128)(2,1)}), bf16[256,1536]{1,0:T(8,128)(2,1)}) %reduce-scatter.5.cloned.1.call-update) | async-done | bytes 786448 | tf_op jit(solution)/shard_map/reduce_scatter | solution.py:141
  106.7 1.7 multiply_reduce_fusion.1
  109.0 2.5 multiply_convert_fusion.3
  112.2 28.0 %all-gather.9.cloned.1.call-done = bf16[1024,1536]{1,0:T(8,128)(2,1)} async-done(((bf16[256,1536]{1,0:T(8,128)(2,1)}), bf16[1024,1536]{1,0:T(8,128)(2,1)}) %all-gather.9.cloned.1.call-update) | async-done | bytes 3145744 | tf_op jit(solution)/shard_map/all_gather | solution.py:148
  140.2 8.4 fusion.58
  148.6 4.9 fusion.57
  153.5 16.6 %all-gather.11.cloned.1.call-done = bf16[1024,1536]{1,0:T(8,128)(2,1)} async-done(((bf16[256,1536]{1,0:T(8,128)(2,1)}), bf16[1024,1536]{1,0:T(8,128)(2,1)}) %all-gather.11.cloned.1.call-update) | async-done | bytes 3145744 | tf_op jit(solution)/shard_map/all_gather | solution.py:163
  170.2 9.5 %multiply_convert_fusion = (bf16[1024,1024]{1,0:T(8,128)(2,1)S(1)}, bf16[1024,1024]{1,0:T(8,128)(2,1)S(1)}, bf16[1024,1024]{1,0:T(8,128)(2,1)}) fusion(f32[1024,1024]{1,0:T(8,128)} %fusion.57, f32[1024,1024]{1,0:T(8,128)} %fusion.58, bf16[1024,1536]{1,0:T(8,128)(2,1)} %all-gather.11.cloned.1.call-done, bf16[1024,1536]{1,0:T(8,128)(2,1)S(1)} %copy-done), kind=kOutput, calls=%fused_computation.15 | convolution fusion | flops 3236954112 | bytes 20971520 | tf_op jit(solution)/shard_map/dot_general | solution.py:52
  179.7 3.5 fusion.59
  183.2 4.9 add_convert_fusion.1
  188.2 38.0 %reduce-scatter.9.cloned.1.call-done = bf16[256,1536]{1,0:T(8,128)(2,1)} async-done(((bf16[1024,1536]{1,0:T(8,128)(2,1)}), bf16[256,1536]{1,0:T(8,128)(2,1)}) %reduce-scatter.9.cloned.1.call-update) | async-done | bytes 786448 | tf_op jit(solution)/shard_map/reduce_scatter | solution.py:172
  226.1 2.2 fusion.25
  228.3 0.6 copy-done.38
  228.9 3.5 fusion.53
  232.9 1.4 log_add_fusion
  234.2 26.9 %all-gather.13.cloned.1.call-done = bf16[1024,1536]{1,0:T(8,128)(2,1)} async-done(((bf16[256,1536]{1,0:T(8,128)(2,1)}), bf16[1024,1536]{1,0:T(8,128)(2,1)}) %all-gather.13.cloned.1.call-update) | async-done | bytes 3145744 | tf_op jit(solution)/shard_map/all_gather | solution.py:180
  261.1 3.8 convolution_convert_fusion.9
  265.2 8.2 fusion.38
  273.5 9.5 %fusion.1 = bf16[2,2,1024,1024]{2,3,1,0:T(8,128)(2,1)S(1)} fusion(f32[2,1024,1024,2]{2,1,3,0:T(8,128)} %copy-done.1, f32[2,2,1024]{2,1,0:T(2,128)S(1)} %bitcast.155, f32[2,2,1024]{2,1,0:T(2,128)S(1)} %copy-done.35, pred[1024,1024]{0,1:T(8,128)(4,1)S(1)} %copy-done.7, bf16[1024,2,96,1]{0,2,3,1:T(8,128)(2,1)S(1)} %bitcast.157, ...), kind=kOutput, calls=%fused_computation.2 | convolution fusion | flops 830472192 | bytes 27426816 | tf_op jit(solution)/shard_map/while/body/eval_jaxpr/lkgd,mkd->kglm/dot_general | solution.py:86
  282.9 2.7 convolution_bitcast_fusion
  285.7 1.5 convolution_multiply_fusion
  287.4 0.8 copy-done.5
  289.2 0.7 copy-done.21
  289.8 1.9 fusion.60
  291.9 1.0 fusion.61
  293.0 2.7 add_convert_fusion
  295.8 6.4 convolution_convert_fusion.4
  302.5 8.7 convolution_convert_fusion.1
  311.1 4.9 convolution_convert_fusion.2
  316.0 4.8 convolution_convert_fusion.3
  320.9 1.6 convolution_convert_fusion.8
  322.5 1.6 convolution_convert_fusion.7
  324.1 2.4 convolution_convert_fusion.5
  326.6 4.9 convolution_convert_fusion.6
  331.6 2.2 reduce-scatter.11.cloned.1.call-done
  333.8 1.8 fusion.29
  335.6 40.0 %all-reduce = (f32[1536]{0:T(1024)}, f32[1536]{0:T(1024)}) all-reduce(f32[1536]{0:T(1024)S(1)} %get-tuple-element.51, f32[1536]{0:T(1024)S(1)} %get-tuple-element.49), channel_id=1, replica_groups=mesh['dp'=8,'tensor'=4] {'dp','tensor'}, use_global_device_ids=true, to_apply=%region_12.13 | all-reduce | flops 3072 | bytes 24576 | tf_op jit(solution)/shard_map/psum | solution.py:213
  375.6 4.9 fusion.20
  380.5 363.5 %all-reduce.4.cloned.1.call-done = (bf16[1536,192]{0,1:T(8,128)(2,1)}, bf16[1536,192]{0,1:T(8,128)(2,1)}, bf16[384,1536]{1,0:T(8,128)(2,1)}, bf16[1536,1024]{1,0...) async-done(((bf16[1536,192]{0,1:T(8,128)(2,1)}, bf16[1536,192]{0,1:T(8,128)(2,1)}, bf16[384,1536]{1,0:T(8,128)(2,1)}, bf16[1536,1024]{1,0:T(8,128)(2,1)}, ...) | async-done | bytes 11796496 | tf_op jit(solution)/shard_map/psum | solution.py:217
  744.1 2.4 convert_element_type.196
  746.4 2.2 convert_element_type.198
  748.6 1.7 convert_element_type.200
  750.3 3.8 convert_element_type.202
  754.1 3.5 convert_element_type.204
  757.6 3.6 convert_element_type.206
  761.2 121.7 %all-gather.15.cloned.1.call-done = bf16[12288,384]{1,0:T(8,128)(2,1)} async-done(((bf16[1536,384]{1,0:T(8,128)(2,1)}), bf16[12288,384]{1,0:T(8,128)(2,1)}) %all-gather.15.cloned.1.call-update) | async-done | bytes 9437200 | tf_op jit(solution)/shard_map/all_gather | solution.py:216
  882.9 6.3 reduce_sum.94
  889.2 2.8 convert_element_type.194
  (138 shorter events, 5.8 us)
Async XLA Ops:
  7.2 163.0 %copy-start = (bf16[1024,1536]{1,0:T(8,128)(2,1)S(1)}, bf16[1024,1536]{1,0:T(8,128)(2,1)}, u32[]{:S(2)}) copy-start(bf16[1024,1536]{1,0:T(8,128)(2,1)} %param.20) | copy-start | bytes 9437188
  7.2 35.8 %all-gather.7.cloned.1.call-start = ((), (), s32[]{:S(2)}) async-start(), calls=%async_computation.4 | async-start | bytes 3932160 | tf_op jit(solution)/shard_map/all_gather | solution.py:118
  8.8 0.6 copy-start.36
  11.6 95.1 %reduce-scatter.5.cloned.1.call-start = ((), (), s32[]{:S(2)}) async-start(), calls=%async_computation.5 | async-start | bytes 3932160 | tf_op jit(solution)/shard_map/reduce_scatter | solution.py:141
  43.0 3.4 copy-start.2
  43.0 3.4 copy-start.20
  47.9 1.0 copy-start.4
  48.9 1.4 copy-start.6
  49.1 4.2 copy-start.14
  50.3 3.1 copy-start.9
  53.4 5.8 copy-start.1
  53.4 5.8 copy-start.31
  53.4 3.7 copy-start.26
  57.1 7.2 copy-start.32
  58.3 6.0 copy-start.47
  59.2 6.0 copy-start.46
  64.3 0.9 copy-start.23
  68.7 40.3 %copy-start.29 = (f32[1536]{0:T(1024)S(1)}, f32[1536]{0:T(1024)}, u32[]{:S(2)}) copy-start(f32[1536]{0:T(1024)} %param.13) | copy-start | bytes 18436
  68.7 71.5 %all-gather.9.cloned.1.call-start = ((), (), s32[]{:S(2)}) async-start(), calls=%async_computation.6 | async-start | bytes 3932160 | tf_op jit(solution)/shard_map/all_gather | solution.py:148
  108.4 0.5 copy-start.33
  111.5 58.6 %all-gather.11.cloned.1.call-start = ((), (), s32[]{:S(2)}) async-start(), calls=%async_computation.8 | async-start | bytes 3932160 | tf_op jit(solution)/shard_map/all_gather | solution.py:163
  112.1 114.0 %reduce-scatter.9.cloned.1.call-start = ((), (), s32[]{:S(2)}) async-start(), calls=%async_computation.9 | async-start | bytes 3932160 | tf_op jit(solution)/shard_map/reduce_scatter | solution.py:172
  140.2 8.4 copy-start.40
  140.2 8.4 copy-start.43
  170.2 9.5 %copy-start.41 = (bf16[1536,1024]{1,0:T(8,128)(2,1)S(1)}, bf16[1536,1024]{1,0:T(8,128)(2,1)}, u32[]{:S(2)}) copy-start(bf16[1536,1024]{1,0:T(8,128)(2,1)} %param.18) | copy-start | bytes 9437188
  179.7 3.5 copy-start.49
  179.7 3.5 copy-start.51
  179.7 3.5 copy-start.42
  188.1 73.0 %all-gather.13.cloned.1.call-start = ((), (), s32[]{:S(2)}) async-start(), calls=%async_computation.10 | async-start | bytes 3932160 | tf_op jit(solution)/shard_map/all_gather | solution.py:180
  228.3 0.6 copy-start.38
  232.4 101.4 %reduce-scatter.11.cloned.1.call-start = ((), (), s32[]{:S(2)}) async-start(), calls=%async_computation.11 | async-start | bytes 3932160 | tf_op jit(solution)/shard_map/reduce_scatter | solution.py:205
  261.1 3.8 copy-start.24
  261.1 4.1 copy-start.7
  261.1 4.1 copy-start.35
  265.2 8.3 copy-start.48
  273.4 19.5 %copy-start.18 = (bf16[2,96,1024]{2,1,0:T(8,128)(2,1)}, bf16[2,96,1024]{2,1,0:T(8,128)(2,1)S(1)}, u32[]{:S(2)}) copy-start(bf16[2,96,1024]{2,1,0:T(8,128)(2,1)S(1)} %fusion.38) | copy-start | bytes 1179652
  273.4 9.5 %copy-start.10 = (bf16[1024,2,2,96]{0,3,2,1:T(8,128)(2,1)S(1)}, bf16[1024,2,2,96]{0,3,2,1:T(8,128)(2,1)}, u32[]{:S(2)}) copy-start(bf16[1024,2,2,96]{0,3,2,1:T(8,128)(2,1)} %copy-done.9) | copy-start | bytes 2359300
  282.9 2.7 copy-start.15
  285.7 1.5 copy-start.17
  287.2 1.0 copy-start.5
  288.5 1.3 copy-start.21
  289.8 1.9 copy-start.8
  289.8 1.9 copy-start.16
  289.8 2.1 copy-start.28
  291.9 1.1 copy-start.27
  295.7 79.9 %reduce-scatter.7.cloned.1.call-start = ((), (), s32[]{:S(2)}) async-start(), calls=%async_computation.7 | async-start | bytes 3932160 | tf_op jit(solution)/shard_map/reduce_scatter | solution.py:156
  302.2 441.9 %all-reduce.4.cloned.1.call-start = ((), (), s32[]{:S(2)}) async-start(), calls=%async_computation.13 | async-start | bytes 23592960 | tf_op jit(solution)/shard_map/psum | solution.py:217
  302.4 8.7 copy-start.44
  302.4 8.7 copy-start.52
  311.1 4.9 copy-start.50
  316.0 4.9 copy-start.3
  320.9 1.6 copy-start.19
  320.9 3.2 copy-start.25
  320.9 3.2 copy-start.45
  326.5 7.2 copy-start.30
  326.6 7.2 copy-start.37
  326.6 49.0 %copy-start.34 = (f32[256]{0:T(256)S(1)}, f32[256]{0:T(256)}, u32[]{:S(2)}) copy-start(f32[256]{0:T(256)} %copy-done.33) | copy-start | bytes 3076
  326.6 49.0 %copy-start.39 = (f32[256]{0:T(256)S(1)}, f32[256]{0:T(256)}, u32[]{:S(2)}) copy-start(f32[256]{0:T(256)} %copy-done.38) | copy-start | bytes 3076
  326.6 556.3 %all-gather.15.cloned.1.call-start = ((), (), s32[]{:S(2)}) async-start(), calls=%async_computation.12 | async-start | bytes 10616832 | tf_op jit(solution)/shard_map/all_gather | solution.py:216
  744.1 4.6 copy-start.22
  744.1 6.3 copy-start.13
  750.3 3.8 copy-start.12
  754.1 3.5 copy-start.11
Sparse Core Ops, SparseCore 0:
  11.7 31.2 all-gather.6
  68.8 37.8 reduce-scatter.4
  111.7 28.4 all-gather.8
  141.6 28.4 all-gather.10
  188.2 37.8 reduce-scatter.8
  232.5 28.5 all-gather.12
  295.8 37.8 reduce-scatter.10
  336.9 38.2 reduce-scatter.6
  381.5 362.4 all-reduce.3
  746.7 136.1 all-gather.14
